TPU v7x, 256 devices: a whole 4x4x8 slice. The times are simulated.
256 devices in a mesh: tm: 4 (over x_hi, core), space: 64 (over z, x_lo, y).
Axes of the slice: x: 4 (x_hi: 2, x_lo: 2; x = x_hi * 2 + x_lo), y: 4, z: 8, core: 2. Of those that a mesh axis runs over, the one named last changes fastest.
Arguments:
- queries: bfloat16 [4, 4, 64, 32, 1536], P('tm', None, 'space'), may hold values from -30 to 30
- key_states: bfloat16 [4, 4, 64, 32, 1536], P('tm', None, 'space'), may hold values from -30 to 30, as said below
- value_states: bfloat16 [4, 4, 64, 32, 1536], P('tm', None, 'space'), may hold values from -6 to 6
- conv_weight: float32 [3, 3, 3, 1536], replicated, may hold values from -0.3125 to 0.3125
Outputs:
- mixed: bfloat16 [4, 4, 64, 32, 1536], P('tm', None, 'space')
Inputs may be any that keep to these rules, and one draw needn't show every extreme that they name: `key_states`: entries are real-valued keys.
All inputs are finite; a program needn't handle non-finite values.
Results may differ from a plain program's by a relative error of at most 0.0088.
Values may be sent and summed in bfloat16 or wider, within the bound.
No kernel may reach another device: no remote copies, remote signals or barrier semaphores. Data moves between devices by JAX's collectives and lax.ppermute only.
A program may use at most 192 MiB of HBM per device.

v0:
```python
import math
import jax
import jax.numpy as jnp
from jax import lax
from jax.sharding import PartitionSpec as P

HEADS = 24
HEAD_DIM = 64
D = 1536
FRAMES = 4
ROWS_DEV = 1
COLUMNS = 32
AGENT_DEV = 4


def extended(cells, sides, width):
    for axis, dim in sides:
        count = lax.axis_size(axis)
        ends = count - 1
        head = lax.slice_in_dim(cells, 0, width, axis=dim)
        tail = lax.slice_in_dim(cells, cells.shape[dim] - width, cells.shape[dim], axis=dim)
        cells = jnp.concatenate(
            [
                lax.ppermute(tail, axis, [(i, (i + 1) % count) for i in range(ends)]),
                cells,
                lax.ppermute(head, axis, [((i + 1) % count, i) for i in range(ends)]),
            ],
            axis=dim,
        )
    return cells


def mix_local(window, conv_weight):
    shape = (window.shape[0] - 2, window.shape[1] - 2, window.shape[2] - 2, window.shape[3])
    total = jnp.zeros(shape, jnp.float32)
    for time_off in range(3):
        for row_off in range(3):
            for col_off in range(3):
                piece = window[
                    time_off : time_off + shape[0],
                    row_off : row_off + shape[1],
                    col_off : col_off + shape[2],
                ]
                total = total + piece.astype(jnp.float32) * conv_weight[time_off, row_off, col_off]
    return total


def on_device(queries, key_states, value_states, conv_weight):
    tokens = FRAMES * ROWS_DEV * COLUMNS
    inv_root = HEAD_DIM ** (-0.5)
    per_block = math.gcd(HEADS, 8)
    blocks = HEADS // per_block
    padded = extended(value_states, (("tm", 1), ("space", 2)), 1)
    window = jnp.pad(padded[0], ((0, 0), (0, 0), (1, 1), (0, 0)))
    pooled = jnp.mean(
        queries.reshape(FRAMES, ROWS_DEV, AGENT_DEV, COLUMNS // AGENT_DEV, D),
        axis=(0, 1, 3),
        dtype=jnp.float32,
    )
    agents = lax.all_gather(pooled.astype(jnp.bfloat16), "space", axis=0, tiled=True)
    count = agents.shape[0]
    agent_heads = agents.reshape(count, HEADS, HEAD_DIM)
    query_heads = queries.reshape(tokens, HEADS, HEAD_DIM)
    key_heads = key_states.reshape(tokens, HEADS, HEAD_DIM)
    value_heads = value_states.reshape(tokens, HEADS, HEAD_DIM)

    def agent_block(index):
        start = index * per_block
        agent_part = lax.dynamic_slice_in_dim(agent_heads, start, per_block, 1)
        key_part = lax.dynamic_slice_in_dim(key_heads, start, per_block, 1)
        value_part = lax.dynamic_slice_in_dim(value_heads, start, per_block, 1)
        scores = (
            jnp.einsum("ahd,nhd->ahn", agent_part, key_part, preferred_element_type=jnp.float32)
            * inv_root
        )
        block_peak = jnp.max(scores, axis=2)
        weights = jnp.exp(scores - block_peak[..., None])
        block_total = jnp.sum(weights, axis=2)
        block_acc = jnp.einsum(
            "ahn,nhd->ahd",
            weights.astype(jnp.bfloat16),
            value_part,
            preferred_element_type=jnp.float32,
        )
        return (block_peak, block_total, block_acc)

    peaks, totals, accs = lax.map(agent_block, jnp.arange(blocks, dtype=jnp.int32))
    local_peak = peaks.transpose(1, 0, 2).reshape(count, HEADS)
    local_total = totals.transpose(1, 0, 2).reshape(count, HEADS)
    local_acc = accs.transpose(1, 0, 2, 3).reshape(count, HEADS, HEAD_DIM)
    peak = lax.pmax(local_peak, "space")
    rescale = jnp.exp(local_peak - peak)
    total_sum, acc_sum = lax.psum((local_total * rescale, local_acc * rescale[..., None]), "space")
    agent_values = (acc_sum / total_sum[..., None]).astype(jnp.bfloat16)

    def query_block(index):
        start = index * per_block
        query_part = lax.dynamic_slice_in_dim(query_heads, start, per_block, 1)
        agent_part = lax.dynamic_slice_in_dim(agent_heads, start, per_block, 1)
        values_part = lax.dynamic_slice_in_dim(agent_values, start, per_block, 1)
        query_scores = (
            jnp.einsum("nhd,ahd->hna", query_part, agent_part, preferred_element_type=jnp.float32)
            * inv_root
        )
        probs = jax.nn.softmax(query_scores, axis=-1).astype(jnp.bfloat16)
        return jnp.einsum("hna,ahd->nhd", probs, values_part, preferred_element_type=jnp.float32)

    outputs = lax.map(query_block, jnp.arange(blocks, dtype=jnp.int32))
    attended = outputs.transpose(1, 0, 2, 3).reshape(FRAMES, ROWS_DEV, COLUMNS, D)
    local_mix = mix_local(window, conv_weight)
    mixed = (attended + local_mix).astype(jnp.bfloat16)
    return mixed.reshape(value_states.shape)


def solution(mesh):
    return jax.shard_map(
        on_device,
        mesh=mesh,
        in_specs=(
            P("tm", None, "space", None, None),
            P("tm", None, "space", None, None),
            P("tm", None, "space", None, None),
            P(),
        ),
        out_specs=P("tm", None, "space", None, None),
        check_vma=False,
    )
```

profile of v0, /device:TPU:4, one launch (start us, length us, event | category | flops | bytes accessed | tf_op | source)
XLA Modules:
  0.0 1130.5 jit_solution(9148870399939223260)
XLA Ops:
  6.5 0.0 all-reduce.3.cloned.1.call-start
  6.5 1.6 reshape.95
  8.2 0.5 copy.36
  8.7 0.0 copy-done.1
  8.7 0.1 convert_reduce_fusion
  8.7 0.1 bitcast_reduce_fusion
  8.8 162.9 %all-gather = bf16[64,4,1536]{2,1,0:T(4,128)(2,1)S(1)} all-gather(bf16[1,4,1536]{2,1,0:T(4,128)(2,1)S(1)} %fusion.47), channel_id=1, replica_groups=mesh['tm'=4,'space'=64] {'space'}, dimensions={0}, use_global_device_ids=true | all-gather | bytes 798720 | tf_op jit(solution)/shard_map/all_gather | solution.py:60
  171.7 0.8 reshape.96
  172.5 0.0 copy-start
  172.6 1.0 copy.37
  173.6 0.0 copy-done
  173.6 0.4 reshape.97
  174.0 0.5 copy.38
  174.5 9.1 while.24
  174.5 0.7 dynamic_slice.74
  175.9 0.4 fusion.69
  176.3 0.2 fusion.70
  176.5 1.1 fusion.71
  177.6 0.7 dynamic_slice.74
  178.9 0.4 fusion.69
  179.3 0.2 fusion.70
  179.5 1.1 fusion.71
  180.6 0.7 dynamic_slice.74
  182.0 0.4 fusion.69
  182.3 0.2 fusion.70
  182.5 1.1 fusion.71
  183.6 302.7 %pmax.7 = f32[256,24]{0,1:T(8,128)S(1)} all-reduce(f32[256,24]{0,1:T(8,128)S(1)} %bitcast.68), channel_id=1, replica_groups=mesh['tm'=4,'space'=64] {'space'}, use_global_device_ids=true, to_apply=%region_6.7 | all-reduce | flops 6144 | bytes 49152 | tf_op jit(solution)/shard_map/pmax | solution.py:91
  486.4 0.6 bitcast_multiply_fusion.1
  487.0 2.8 bitcast_multiply_fusion
  489.7 0.0 all-reduce.3.cloned.1.call-update
  489.8 2.1 collective-permute-start.1
  491.8 2.4 collective-permute-start
  494.2 5.5 collective-permute-done.1
  499.8 1.9 collective-permute-done
  501.6 0.1 pad_maximum_fusion
  501.7 0.0 copy-done.3
  501.7 1.3 collective-permute-start.3
  503.0 0.0 copy-done.4
  503.0 5.4 collective-permute-start.2
  508.4 0.0 copy-done.2
  508.4 0.4 reshape.101
  508.9 1.2 copy.39
  510.1 302.9 %psum.15 = f32[256,24]{0,1:T(8,128)} all-reduce(f32[256,24]{0,1:T(8,128)} %get-tuple-element.182), channel_id=1, replica_groups=mesh['tm'=4,'space'=64] {'space'}, use_global_device_ids=true, to_apply=%region_8.9 | all-reduce | flops 6144 | bytes 49152 | tf_op jit(solution)/shard_map/psum | solution.py:93
  813.0 1.6 slice_reduce_fusion.25
  814.6 2.0 slice_reduce_fusion.26
  816.6 0.0 collective-permute-done.3
  816.6 0.0 collective-permute-done.2
  816.6 1.4 maximum_bitcast_fusion
  818.0 279.5 %all-reduce.3.cloned.1.call-done = f32[256,24,64]{0,2,1:T(8,128)} async-done(((f32[256,24,64]{0,2,1:T(8,128)}), f32[256,24,64]{0,2,1:T(8,128)}) %all-reduce.3.cloned.1.call-update) | async-done | bytes 1572880 | tf_op jit(solution)/shard_map/psum | solution.py:93
  1097.5 1.6 divide_convert_fusion.2
  1099.1 15.7 %while.25 = (s32[]{:T(128)}, f32[3,128,8,64]{1,3,2,0:T(8,128)}, s32[3]{0:T(128)S(1)}, bf16[256,24,64]{0,2,1:T(8,128)(2,1)S(1)}, bf16[128,24,64]{0,2,1:T(8,128)(2...) while((s32[]{:T(128)}, f32[3,128,8,64]{1,3,2,0:T(8,128)}, ...), condition=%wide.region_12.13_spmd, body=%wide.region_9.12_spmd.sunk | while | flops 102499840 | bytes 1322151 | solution.py:108
  1099.1 0.6 dynamic_slice.80
  1100.4 1.6 fusion.77
  1102.0 2.4 fusion.78
  1104.4 0.6 dynamic_slice.80
  1105.6 1.6 fusion.77
  1107.2 2.4 fusion.78
  1109.6 0.6 dynamic_slice.80
  1110.9 1.6 fusion.77
  1112.4 2.4 fusion.78
  1114.9 1.7 copy.41
  1116.8 1.3 reshape.102
  1118.0 0.0 copy-done.8
  1118.3 5.4 fusion.46
  (62 shorter events, 0.2 us)
Async XLA Ops:
  6.5 2.1 copy-start.1
  6.5 1091.0 %all-reduce.3.cloned.1.call-start = ((), (), s32[]{:S(2)}) async-start(), calls=%async_computation | async-start | bytes 3145728 | tf_op jit(solution)/shard_map/psum | solution.py:93
  172.5 1.0 copy-start
  489.7 18.7 %copy-start.2 = (bf16[1,4,1,32,1536]{4,3,2,1,0:T(8,128)(2,1)S(1)}, bf16[1,4,1,32,1536]{4,3,2,1,0:T(8,128)(2,1)}, u32[]{:S(2)}) copy-start(bf16[1,4,1,32,1536]{4,3,2,1,0:T(8,128)(2,1)} %param.8) | copy-start | bytes 1179652
  489.8 10.0 collective-permute-start.1
  491.8 9.8 collective-permute-start
  499.8 1.9 copy-start.3
  501.6 1.4 copy-start.4
  501.7 314.9 %collective-permute-start.3 = (bf16[1,6,1,32,1536]{4,3,1,2,0:T(8,128)(2,1)S(1)}, bf16[1,6,1,32,1536]{4,3,1,2,0:T(8,128)(2,1)S(1)}, u32[]{:S(2)}, u32[]{:S(2)}) collective-permute-start(bf16[1,6,1,32,1536]{4,3,1,2,0:T(8,128)(2,1)S(1)} %pad_maximum_fusion), channel_id=1, source_target_pairs={{1,0},{2,1},{3,2},{4,3},{5,4},{6,5},{7,6},{8,7},{9,8},{10,9},{11,1... | collective-permute-start | bytes 1769480 | tf_op jit(solution)/shard_map/ppermute | solution.py:26
  503.0 313.6 %collective-permute-start.2 = (bf16[1,6,1,32,1536]{4,3,1,2,0:T(8,128)(2,1)S(1)}, bf16[1,6,1,32,1536]{4,3,1,2,0:T(8,128)(2,1)}, u32[]{:S(2)}, u32[]{:S(2)}) collective-permute-start(bf16[1,6,1,32,1536]{4,3,1,2,0:T(8,128)(2,1)S(1)} %pad_maximum_fusion), channel_id=1, source_target_pairs={{0,1},{1,2},{2,3},{3,4},{4,5},{5,6},{6,7},{7,8},{8,9},{9,10},{10,1... | collective-permute-start | bytes 1769480 | tf_op jit(solution)/shard_map/ppermute | solution.py:24
  1116.5 1.5 copy-start.5
  1116.5 1.5 copy-start.6
  1116.6 1.5 copy-start.7
  1116.6 1.5 copy-start.8
  1116.6 1.5 copy-start.9
  1116.6 1.5 copy-start.10
  1116.6 1.5 copy-start.11
  1116.6 1.5 copy-start.12
  1116.6 1.5 copy-start.13
  1116.6 1.5 copy-start.14
  1116.6 1.5 copy-start.15
  1116.6 1.5 copy-start.16
  1116.7 1.5 copy-start.17
  1116.7 1.5 copy-start.18
  1116.7 1.5 copy-start.19
  1116.7 1.5 copy-start.20
  1116.7 1.5 copy-start.21
  1116.7 1.5 copy-start.22
  1116.7 1.5 copy-start.23
  1116.7 1.5 copy-start.24
  1116.7 1.5 copy-start.25
  1116.7 1.5 copy-start.26
  1116.8 1.5 copy-start.27
  1116.8 1.5 copy-start.28
Sparse Core Ops, SparseCore 0:
  489.9 607.6 all-reduce.2
where the time goes:
time: 1130 us
  blocking collectives  769 us (68%)
  waiting for transfers between devices  287 us (25%)
  local copies, waits for them, and re-layouts  17.1 us (2%)
  matrix products  16.4 us (1%)
  between operations  13.9 us (1%)
  other arithmetic  12.4 us (1%)
    psum x1, blocking collectives, on_device(): lax.psum((local_total * rescale, local_acc * rescale[..., None]), 'space')  303 us
    pmax x1, blocking collectives, on_device(): peak = lax.pmax(local_peak, 'space')  303 us
    psum x1, waiting for transfers between devices, on_device(): lax.psum((local_total * rescale, local_acc * rescale[..., None]), 'space')  280 us
    all_gather x1, blocking collectives, on_device(): lax.all_gather(pooled.astype(jnp.bfloat16), 'space', axis=0, tiled=True)  163 us
  transfers between devices with their start and end apart: 5, of which 3 were waited for; matrix products, arithmetic and copies ran while one was open for 1% of the time, Pallas kernels for 0%

commit v1 on v0

--- a/solution.py
+++ b/solution.py
@@ -57,7 +57,12 @@
         axis=(0, 1, 3),
         dtype=jnp.float32,
     )
-    agents = lax.all_gather(pooled.astype(jnp.bfloat16), "space", axis=0, tiled=True)
+    agents = jnp.concatenate(
+        lax.all_to_all(
+            jnp.stack([pooled.astype(jnp.bfloat16)] * lax.axis_size("space")), "space", 0, 0
+        ),
+        axis=0,
+    )
     count = agents.shape[0]
     agent_heads = agents.reshape(count, HEADS, HEAD_DIM)
     query_heads = queries.reshape(tokens, HEADS, HEAD_DIM)

time: 1130 us -> 1010 us (0.89)
  blocking collectives: 769 us -> 611 us
  waiting for transfers between devices: 287 us -> 306 us
  starting transfers between devices: 11.1 us -> 23.9 us
    all_gather x1 -> x0, blocking collectives: 163 us -> none  [on_device(): lax.all_gather(pooled.astype(jnp.bfloat16), 'space', axis=0, tiled=True)]
    all_to_all x0 -> x1, waiting for transfers between devices: none -> 20.4 us  [on_device(): lax.all_to_all(jnp.stack([pooled.astype(jnp.bfloat16)] * lax.axis_size('s...]
    all_to_all x0 -> x1, starting transfers between devices: none -> 12.7 us  [on_device(): lax.all_to_all(jnp.stack([pooled.astype(jnp.bfloat16)] * lax.axis_size('s...]
  transfers between devices with their start and end apart: 5 -> 6, of which waited for: 3 -> 6; matrix products, arithmetic and copies ran while one was open for 1% -> 1% of each run, Pallas kernels for 0% -> 0%
where the time goes in v1:
time: 1010 us
  blocking collectives  611 us (60%)
  waiting for transfers between devices  306 us (30%)
  starting transfers between devices  23.9 us (2%)
  matrix products  19.1 us (2%)
  local copies, waits for them, and re-layouts  17.6 us (2%)
  between operations  14 us (1%)
  other arithmetic  13.5 us (1%)
    psum x1, blocking collectives, on_device(): lax.psum((local_total * rescale, local_acc * rescale[..., None]), 'space')  306 us
    pmax x1, blocking collectives, on_device(): peak = lax.pmax(local_peak, 'space')  305 us
    psum x1, waiting for transfers between devices, on_device(): lax.psum((local_total * rescale, local_acc * rescale[..., None]), 'space')  278 us
    all_to_all x1, waiting for transfers between devices, on_device(): lax.all_to_all(jnp.stack([pooled.astype(jnp.bfloat16)] * lax.axis_size('s...  20.4 us
  transfers between devices with their start and end apart: 6, of which 6 were waited for; matrix products, arithmetic and copies ran while one was open for 1% of the time, Pallas kernels for 0%

profile of v1, /device:TPU:4, one launch (start us, length us, event | category | flops | bytes accessed | tf_op | source)
XLA Modules:
  0.0 1008.7 jit_solution(16076439362693872958)
XLA Ops:
  6.5 1.1 convert_reduce_fusion
  7.7 0.1 bitcast_reduce_fusion
  7.7 1.1 stack.2
  8.8 12.7 %all-to-all-start = ((bf16[64,4,1536]{2,1,0:T(4,128)(2,1)}), bf16[64,4,1536]{2,1,0:T(4,128)(2,1)S(1)}, u32[]{:S(2)}, u32[]{:S(2)}) async-start(bf16[64,4,1536]{2,1,0:T(4,128)(2,1)} %stack.2), calls=%async_computation | async-start | bytes 1572864 | tf_op jit(solution)/shard_map/all_to_all | solution.py:61
  21.6 0.0 copy-start
  21.6 0.0 all-reduce.3.cloned.1.call-start
  21.7 0.4 reshape.94
  22.1 0.5 copy.25
  22.6 0.4 reshape.95
  23.1 1.2 copy.27
  24.3 20.4 %all-to-all-done = bf16[64,4,1536]{2,1,0:T(4,128)(2,1)S(1)} async-done(((bf16[64,4,1536]{2,1,0:T(4,128)(2,1)}), bf16[64,4,1536]{2,1,0:T(4,128)(2,1)S(1)}, u32[]{:S(2)}, u32[]{:S(2)}) %all-to-all-start) | async-done | bytes 786464 | tf_op jit(solution)/shard_map/all_to_all | solution.py:61
  44.7 0.8 reshape_reshape.3
  45.5 1.0 copy.26
  46.5 11.1 %while.24 = (s32[]{:T(128)}, f32[3,256,8]{1,2,0:T(8,128)S(1)}, f32[3,256,8]{1,2,0:T(8,128)S(1)}, f32[3,256,8,64]{1,3,2,0:T(8,128)}, s32[3]{0:T(128)S(1)}, /*inde...) while((s32[]{:T(128)}, f32[3,256,8]{1,2,0:T(8,128)S(1)}, ...), condition=%wide.region_5.6_spmd, body=%wide.region_2.5_spmd.sunk | while | flops 68677632 | bytes 4261059 | solution.py:92
  46.5 0.6 dynamic_slice.74
  47.6 0.4 fusion.68
  48.0 0.2 fusion.69
  48.2 2.0 fusion.70
  50.2 0.6 dynamic_slice.74
  51.3 0.4 fusion.68
  51.7 0.2 fusion.69
  51.8 2.0 fusion.70
  53.9 0.6 dynamic_slice.74
  55.0 0.4 fusion.68
  55.3 0.2 fusion.69
  55.5 2.0 fusion.70
  57.6 305.1 %pmax.7 = f32[256,24]{0,1:T(8,128)S(1)} all-reduce(f32[256,24]{0,1:T(8,128)S(1)} %bitcast.67), channel_id=1, replica_groups=mesh['tm'=4,'space'=64] {'space'}, use_global_device_ids=true, to_apply=%region_6.7 | all-reduce | flops 6144 | bytes 49152 | tf_op jit(solution)/shard_map/pmax | solution.py:96
  362.6 0.6 bitcast_multiply_fusion.1
  363.3 2.8 bitcast_multiply_fusion
  366.0 0.0 all-reduce.3.cloned.1.call-update
  366.1 2.1 collective-permute-start.1
  368.1 2.4 collective-permute-start
  370.5 3.5 collective-permute-done.1
  374.0 1.6 collective-permute-done
  375.6 0.1 pad_maximum_fusion
  375.7 0.0 copy-done.2
  375.7 1.3 collective-permute-start.3
  377.0 0.0 copy-done.3
  377.0 5.4 collective-permute-start.2
  382.4 0.4 reshape.99
  382.8 1.2 copy.28
  384.0 1.7 slice_reduce_fusion.25
  385.7 2.2 slice_reduce_fusion.26
  387.9 1.9 collective-permute-done.3
  389.8 1.1 collective-permute-done.2
  390.9 1.4 maximum_bitcast_fusion
  392.3 305.8 %psum.15 = f32[256,24]{0,1:T(8,128)S(1)} all-reduce(f32[256,24]{0,1:T(8,128)} %get-tuple-element.168), channel_id=1, replica_groups=mesh['tm'=4,'space'=64] {'space'}, use_global_device_ids=true, to_apply=%region_8.9 | all-reduce | flops 6144 | bytes 49152 | tf_op jit(solution)/shard_map/psum | solution.py:98
  698.0 277.7 %all-reduce.3.cloned.1.call-done = f32[256,24,64]{0,2,1:T(8,128)} async-done(((f32[256,24,64]{0,2,1:T(8,128)}), f32[256,24,64]{0,2,1:T(8,128)}) %all-reduce.3.cloned.1.call-update) | async-done | bytes 1572880 | tf_op jit(solution)/shard_map/psum | solution.py:98
  975.7 1.6 divide_convert_fusion.2
  977.3 15.7 %while.25 = (s32[]{:T(128)}, f32[3,128,8,64]{1,3,2,0:T(8,128)}, s32[3]{0:T(128)S(1)}, bf16[256,24,64]{0,2,1:T(8,128)(2,1)S(1)}, bf16[128,24,64]{0,2,1:T(8,128)(2...) while((s32[]{:T(128)}, f32[3,128,8,64]{1,3,2,0:T(8,128)}, ...), condition=%wide.region_12.13_spmd, body=%wide.region_9.12_spmd.sunk | while | flops 102499840 | bytes 1322151 | solution.py:113
  977.3 0.6 dynamic_slice.80
  978.6 1.6 fusion.76
  980.2 2.4 fusion.77
  982.6 0.6 dynamic_slice.80
  983.8 1.6 fusion.76
  985.4 2.4 fusion.77
  987.8 0.6 dynamic_slice.80
  989.1 1.6 fusion.76
  990.6 2.4 fusion.77
  993.1 1.7 copy.30
  995.0 1.3 reshape.100
  996.2 0.0 copy-done.6
  996.3 0.0 copy-done.8
  996.5 5.4 fusion.46
  (64 shorter events, 0.2 us)
Async XLA Ops:
  6.5 15.1 %copy-start.4 = (bf16[1,4,1,32,1536]{4,3,2,1,0:T(8,128)(2,1)S(1)}, bf16[1,4,1,32,1536]{4,3,2,1,0:T(8,128)(2,1)}, u32[]{:S(2)}) copy-start(bf16[1,4,1,32,1536]{4,3,2,1,0:T(8,128)(2,1)} %param.9) | copy-start | bytes 1179652
  8.8 35.8 %all-to-all-start = ((bf16[64,4,1536]{2,1,0:T(4,128)(2,1)}), bf16[64,4,1536]{2,1,0:T(4,128)(2,1)S(1)}, u32[]{:S(2)}, u32[]{:S(2)}) async-start(bf16[64,4,1536]{2,1,0:T(4,128)(2,1)} %stack.2), calls=%async_computation | async-start | bytes 1572864 | tf_op jit(solution)/shard_map/all_to_all | solution.py:61
  21.6 1.1 copy-start
  21.6 954.2 %all-reduce.3.cloned.1.call-start = ((), (), s32[]{:S(2)}) async-start(), calls=%async_computation.1 | async-start | bytes 3145728 | tf_op jit(solution)/shard_map/psum | solution.py:98
  366.0 16.4 %copy-start.1 = (bf16[1,4,1,32,1536]{4,3,2,1,0:T(8,128)(2,1)S(1)}, bf16[1,4,1,32,1536]{4,3,2,1,0:T(8,128)(2,1)}, u32[]{:S(2)}) copy-start(bf16[1,4,1,32,1536]{4,3,2,1,0:T(8,128)(2,1)} %param.8) | copy-start | bytes 1179652
  366.1 7.9 collective-permute-start.1
  368.1 7.5 collective-permute-start
  374.0 1.7 copy-start.2
  375.6 1.4 copy-start.3
  375.7 14.1 %collective-permute-start.3 = (bf16[1,6,1,32,1536]{4,3,1,2,0:T(8,128)(2,1)S(1)}, bf16[1,6,1,32,1536]{4,3,1,2,0:T(8,128)(2,1)S(1)}, u32[]{:S(2)}, u32[]{:S(2)}) collective-permute-start(bf16[1,6,1,32,1536]{4,3,1,2,0:T(8,128)(2,1)S(1)} %pad_maximum_fusion), channel_id=1, source_target_pairs={{1,0},{2,1},{3,2},{4,3},{5,4},{6,5},{7,6},{8,7},{9,8},{10,9},{11,1... | collective-permute-start | bytes 1769480 | tf_op jit(solution)/shard_map/ppermute | solution.py:26
  377.0 13.9 %collective-permute-start.2 = (bf16[1,6,1,32,1536]{4,3,1,2,0:T(8,128)(2,1)S(1)}, bf16[1,6,1,32,1536]{4,3,1,2,0:T(8,128)(2,1)}, u32[]{:S(2)}, u32[]{:S(2)}) collective-permute-start(bf16[1,6,1,32,1536]{4,3,1,2,0:T(8,128)(2,1)S(1)} %pad_maximum_fusion), channel_id=1, source_target_pairs={{0,1},{1,2},{2,3},{3,4},{4,5},{5,6},{6,7},{7,8},{8,9},{9,10},{10,1... | collective-permute-start | bytes 1769480 | tf_op jit(solution)/shard_map/ppermute | solution.py:24
  994.7 1.5 copy-start.5
  994.8 1.5 copy-start.6
  994.8 1.5 copy-start.7
  994.8 1.5 copy-start.8
  994.8 1.5 copy-start.9
  994.8 1.5 copy-start.10
  994.8 1.5 copy-start.11
  994.8 1.5 copy-start.12
  994.8 1.5 copy-start.13
  994.8 1.5 copy-start.14
  994.8 1.5 copy-start.15
  994.9 1.5 copy-start.16
  994.9 1.5 copy-start.17
  994.9 1.5 copy-start.18
  994.9 1.5 copy-start.19
  994.9 1.5 copy-start.20
  994.9 1.5 copy-start.21
  994.9 1.5 copy-start.22
  994.9 1.5 copy-start.23
  994.9 1.5 copy-start.24
  994.9 1.5 copy-start.25
  995.0 1.5 copy-start.26
  995.0 1.5 copy-start.27
  995.0 1.5 copy-start.28
Sparse Core Ops, SparseCore 0:
  366.1 609.5 all-reduce.2
